TPU v7x, 512 devices: a whole 4x4x16 slice. The times are simulated.
512 devices in a mesh: row: 8 (over x, core), col: 16 (over z), layer: 4 (over y).
Axes of the slice: x: 4, y: 4, z: 16, core: 2. Of those that a mesh axis runs over, the one named last changes fastest.
Arguments:
- occurrences: bfloat16 [8192, 10240], P(('row', 'col', 'layer')), may hold values from -6 to 6
- idf_weight: float32 [8192], P(('row', 'col', 'layer')), may hold values from 0.25 to 2
- pattern: int32 [64, 80], replicated, may hold values 0 or 1
Outputs:
- margin: bfloat16 [10240, 10240], P('row', 'col')
All inputs are finite; a program needn't handle non-finite values.
Results may differ from a plain program's by a relative error of at most 0.0058.
Values may be sent and summed in bfloat16 or wider, within the bound.
No kernel may reach another device: no remote copies, remote signals or barrier semaphores. Data moves between devices by JAX's collectives and lax.ppermute only.
A program may use at most 64 MiB of HBM per device.

v0:
```python
import math
import jax
import jax.numpy as jnp
from jax import lax
from jax.sharding import PartitionSpec as P


def finish(partial_rows, row_start, col_start, factor):
    row_ids = row_start + lax.broadcasted_iota(jnp.int32, partial_rows.shape, 0)
    col_ids = col_start + lax.broadcasted_iota(jnp.int32, partial_rows.shape, 1)
    result = jnp.where(row_ids == col_ids, jnp.float32(0.0), partial_rows * factor)
    return result.astype(jnp.bfloat16)


def body(occurrences, idf_weight, pattern):
    owned, reads = occurrences.shape
    n_rows = lax.axis_size("row")
    n_cols = lax.axis_size("col")
    n_layers = lax.axis_size("layer")
    factor = 1.0 / math.sqrt(owned * n_rows * n_cols * n_layers)
    owner = lax.axis_index(("row", "col", "layer"))
    block_row = owner * owned // 128
    flags = lax.dynamic_slice_in_dim(pattern, block_row, 1, 0)[0]
    read_mask = jnp.repeat(flags.astype(jnp.float32), 128)
    weighted = (occurrences.astype(jnp.float32) * idf_weight[:, None] * read_mask[None, :]).astype(
        jnp.bfloat16
    )
    piece_len = reads // (n_rows * n_cols)
    reordered = (
        weighted.reshape(owned, n_cols, n_rows, piece_len)
        .transpose(0, 2, 1, 3)
        .reshape(owned, reads)
    )
    row_part, col_part = (
        lax.all_to_all(weighted, ("row", "col"), split_axis=1, concat_axis=0, tiled=True),
        lax.all_to_all(reordered, ("row", "col"), split_axis=1, concat_axis=0, tiled=True),
    )
    column_reads = lax.all_gather(col_part, "row", axis=1, tiled=True)
    partial_tile = lax.dot_general(
        lax.all_gather(row_part, "col", axis=1, tiled=True),
        column_reads,
        (((0,), (0,)), ((), ())),
        preferred_element_type=jnp.float32,
    )
    row_count = partial_tile.shape[0]
    row_start = lax.axis_index("row") * row_count
    col_start = lax.axis_index("col") * partial_tile.shape[1]
    total = lax.psum(partial_tile, "layer")
    return finish(total, row_start, col_start, factor)


def solution(mesh):
    placed = (P(("row", "col", "layer"), None), P(("row", "col", "layer")), P())
    return jax.shard_map(
        body, mesh=mesh, in_specs=placed, out_specs=P("row", "col"), check_vma=False
    )
```

profile of v0, /device:TPU:1, one launch (start us, length us, event | category | flops | bytes accessed | tf_op | source)
XLA Modules:
  0.0 287.5 jit_solution(10885676402827663510)
XLA Ops:
  6.5 0.0 all-gather.5.cloned.1.call-start
  6.5 0.7 convert_bitcast_fusion
  7.2 0.1 broadcast_bitcast_fusion
  7.3 1.1 multiply_convert_fusion
  8.4 0.6 reshape.14
  9.1 0.1 copy.9
  9.2 0.3 copy.10
  9.6 52.5 %all_to_all.38 = bf16[16,128,80]{2,0,1:T(8,128)(2,1)S(1)} all-to-all(bf16[16,128,80]{2,0,1:T(8,128)(2,1)S(1)} %copy.10), channel_id=1, replica_groups=mesh['row'=8,'col'=16,'layer'=4] {'row','col'}, dimensions={1} | all-to-all | bytes 655360 | tf_op jit(solution)/shard_map/all_to_all | solution.py:36
  62.0 0.9 copy.11
  63.0 0.0 all-gather.5.cloned.1.call-update
  63.0 0.0 all-gather.3.cloned.1.call-start
  63.0 0.6 all_to_all.28
  63.7 0.3 copy.7
  64.0 39.7 %all_to_all.39 = bf16[16,128,80]{2,0,1:T(8,128)(2,1)S(1)} all-to-all(bf16[16,128,80]{2,0,1:T(8,128)(2,1)S(1)} %copy.7), channel_id=1, replica_groups=mesh['row'=8,'col'=16,'layer'=4] {'row','col'}, dimensions={1} | all-to-all | bytes 655360 | tf_op jit(solution)/shard_map/all_to_all | solution.py:35
  103.8 0.9 copy.8
  104.7 0.0 all-gather.3.cloned.1.call-update
  104.7 0.0 all-reduce.2.cloned.1.call-start
  104.8 0.0 all-gather.5.cloned.1.call-done
  104.8 67.3 %all-gather.3.cloned.1.call-done = bf16[2048,1280]{0,1:T(8,128)(2,1)} async-done(((bf16[2048,80]{0,1:T(8,128)(2,1)}), bf16[2048,1280]{0,1:T(8,128)(2,1)}) %all-gather.3.cloned.1.call-update) | async-done | bytes 5242896 | tf_op jit(solution)/shard_map/all_gather | solution.py:40
  172.1 9.3 %fusion = f32[1280,640]{1,0:T(8,128)} fusion(bf16[2048,1280]{0,1:T(8,128)(2,1)} %all-gather.3.cloned.1.call-done, bf16[2048,640]{0,1:T(8,128)(2,1)} %all-gather.5.cloned.1.call-done), kind=kOutput, calls=%fused_computation.6 | convolution fusion | flops 3355443200 | bytes 11141120 | tf_op jit(solution)/shard_map/dot_general | solution.py:39
  181.3 0.0 all-reduce.2.cloned.1.call-update
  181.4 96.0 %all-reduce.2.cloned.1.call-done = f32[1280,640]{1,0:T(8,128)} async-done(((f32[1280,640]{1,0:T(8,128)}), f32[1280,640]{1,0:T(8,128)}) %all-reduce.2.cloned.1.call-update) | async-done | bytes 3276816 | tf_op jit(solution)/shard_map/psum | solution.py:48
  277.4 3.5 %select_convert_fusion = bf16[1280,640]{1,0:T(8,128)(2,1)} fusion(f32[1280,640]{1,0:T(8,128)} %all-reduce.2.cloned.1.call-done, s32[640]{0:T(1024)S(1)} %iota_add_fusion.1, s32[1280]{0:T(1024)S(1)} %iota_add_fusion), kind=kLoop, calls=%fused_computation | loop fusion | flops 3276800 | bytes 4922880 | tf_op jit(solution)/shard_map/convert_element_type | solution.py:12
  (2 shorter events, 0.0 us)
Async XLA Ops:
  6.5 98.3 %all-gather.5.cloned.1.call-start = ((), (), s32[]{:S(2)}) async-start(), calls=%async_computation.3 | async-start | bytes 2949120 | tf_op jit(solution)/shard_map/all_gather | solution.py:38
  63.0 109.1 %all-gather.3.cloned.1.call-start = ((), (), s32[]{:S(2)}) async-start(), calls=%async_computation.2 | async-start | bytes 5570560 | tf_op jit(solution)/shard_map/all_gather | solution.py:40
  104.7 172.7 %all-reduce.2.cloned.1.call-start = ((), (), s32[]{:S(2)}) async-start(), calls=%async_computation.4 | async-start | bytes 6553600 | tf_op jit(solution)/shard_map/psum | solution.py:48
Sparse Core Ops, SparseCore 0:
  63.1 29.0 all-gather.4
  104.9 67.1 all-gather.2
  181.5 95.8 all-reduce.1
where the time goes:
time: 288 us; the launch traced here: 287 us
  waiting for transfers between devices  163 us (57%)
  blocking collectives  92.2 us (32%)
  between operations  13.2 us (5%)
  matrix products  9.28 us (3%)
  other arithmetic  5.36 us (2%)
  local copies, waits for them, and re-layouts  4.02 us (1%)
    psum x1, waiting for transfers between devices, body(): total = lax.psum(partial_tile, 'layer')  96 us
    all_gather x1, waiting for transfers between devices, body(): lax.all_gather(row_part, 'col', axis=1, tiled=True)  67.3 us
    all_to_all x1, blocking collectives, body(): lax.all_to_all(reordered, ('row', 'col'), split_axis=1, concat_axis=0, ti...  52.5 us
    all_to_all x1, blocking collectives, body(): lax.all_to_all(weighted, ('row', 'col'), split_axis=1, concat_axis=0, til...  39.7 us
    dot_general x1, matrix products, body(): lax.dot_general(lax.all_gather(row_part, 'col', axis=1, tiled=True), colu...  9.28 us
  transfers between devices with their start and end apart: 3, of which 2 were waited for; matrix products, arithmetic and copies ran while one was open for 0% of the time, Pallas kernels for 0%

commit v1 on v0

--- a/solution.py
+++ b/solution.py
@@ -45,7 +45,11 @@
     row_count = partial_tile.shape[0]
     row_start = lax.axis_index("row") * row_count
     col_start = lax.axis_index("col") * partial_tile.shape[1]
-    total = lax.psum(partial_tile, "layer")
+    n_dev = lax.axis_size("layer")
+    total, far = (partial_tile, 1)
+    while far < n_dev:
+        total = total + lax.ppermute(total, "layer", [(i, i ^ far) for i in range(n_dev)])
+        far = 2 * far
     return finish(total, row_start, col_start, factor)
 
 

time: 288 us -> 336 us (1.17); the launches traced: 287 us -> 329 us
  waiting for transfers between devices: 163 us -> 200 us
  starting transfers between devices: 0.09 us -> 6.96 us
    ppermute x0 -> x2, waiting for transfers between devices: none -> 133 us  [body(): lax.ppermute(total, 'layer', [(i, i ^ far) for i in range(n_dev)])]
    psum x1 -> x0, waiting for transfers between devices: 96 us -> none  [body(): total = lax.psum(partial_tile, 'layer')]
    ppermute x0 -> x2, starting transfers between devices: none -> 6.91 us  [body(): lax.ppermute(total, 'layer', [(i, i ^ far) for i in range(n_dev)])]
  transfers between devices with their start and end apart: 3 -> 4, of which waited for: 2 -> 3; matrix products, arithmetic and copies ran while one was open for 0% -> 0% of each run, Pallas kernels for 0% -> 0%
where the time goes in v1:
time: 336 us; the launch traced here: 329 us
  waiting for transfers between devices  200 us (60%)
  blocking collectives  92.2 us (27%)
  between operations  13.5 us (4%)
  matrix products  7.02 us (2%)
  starting transfers between devices  6.96 us (2%)
  other arithmetic  5.78 us (2%)
  local copies, waits for them, and re-layouts  4 us (1%)
    ppermute x2, waiting for transfers between devices, body(): lax.ppermute(total, 'layer', [(i, i ^ far) for i in range(n_dev)])  133 us
    all_gather x1, waiting for transfers between devices, body(): lax.all_gather(row_part, 'col', axis=1, tiled=True)  67.3 us
    all_to_all x1, blocking collectives, body(): lax.all_to_all(reordered, ('row', 'col'), split_axis=1, concat_axis=0, ti...  52.5 us
    all_to_all x1, blocking collectives, body(): lax.all_to_all(weighted, ('row', 'col'), split_axis=1, concat_axis=0, til...  39.7 us
    dot_general x1, matrix products, body(): lax.dot_general(lax.all_gather(row_part, 'col', axis=1, tiled=True), colu...  7.02 us
    ppermute x2, starting transfers between devices, body(): lax.ppermute(total, 'layer', [(i, i ^ far) for i in range(n_dev)])  6.91 us
  transfers between devices with their start and end apart: 4, of which 3 were waited for; matrix products, arithmetic and copies ran while one was open for 0% of the time, Pallas kernels for 0%

profile of v1, /device:TPU:1, one launch (start us, length us, event | category | flops | bytes accessed | tf_op | source)
XLA Modules:
  0.0 329.5 jit_solution(16987578631194736360)
XLA Ops:
  6.5 0.0 all-gather.5.cloned.1.call-start
  6.5 0.7 convert_bitcast_fusion
  7.2 0.1 broadcast_bitcast_fusion
  7.3 1.1 multiply_convert_fusion
  8.4 0.6 reshape.14
  9.1 0.1 copy.9
  9.2 0.3 copy.10
  9.6 52.5 %all_to_all.38 = bf16[16,128,80]{2,0,1:T(8,128)(2,1)S(1)} all-to-all(bf16[16,128,80]{2,0,1:T(8,128)(2,1)S(1)} %copy.10), channel_id=1, replica_groups=mesh['row'=8,'col'=16,'layer'=4] {'row','col'}, dimensions={1} | all-to-all | bytes 655360 | tf_op jit(solution)/shard_map/all_to_all | solution.py:36
  62.0 0.9 copy.11
  63.0 0.0 all-gather.5.cloned.1.call-update
  63.0 0.0 all-gather.3.cloned.1.call-start
  63.0 0.6 all_to_all.28
  63.7 0.3 copy.7
  64.0 39.7 %all_to_all.39 = bf16[16,128,80]{2,0,1:T(8,128)(2,1)S(1)} all-to-all(bf16[16,128,80]{2,0,1:T(8,128)(2,1)S(1)} %copy.7), channel_id=1, replica_groups=mesh['row'=8,'col'=16,'layer'=4] {'row','col'}, dimensions={1} | all-to-all | bytes 655360 | tf_op jit(solution)/shard_map/all_to_all | solution.py:35
  103.8 0.9 copy.8
  104.7 0.0 all-gather.3.cloned.1.call-update
  104.7 0.0 all-gather.5.cloned.1.call-done
  104.7 67.3 %all-gather.3.cloned.1.call-done = bf16[2048,1280]{0,1:T(8,128)(2,1)} async-done(((bf16[2048,80]{0,1:T(8,128)(2,1)}), bf16[2048,1280]{0,1:T(8,128)(2,1)}) %all-gather.3.cloned.1.call-update) | async-done | bytes 5242896 | tf_op jit(solution)/shard_map/all_gather | solution.py:40
  172.0 7.0 %fusion = f32[1280,640]{1,0:T(8,128)S(1)} fusion(bf16[2048,1280]{0,1:T(8,128)(2,1)} %all-gather.3.cloned.1.call-done, bf16[2048,640]{0,1:T(8,128)(2,1)} %all-gather.5.cloned.1.call-done), kind=kOutput, calls=%fused_computation.6 | convolution fusion | flops 3355443200 | bytes 11141120 | tf_op jit(solution)/shard_map/dot_general | solution.py:39
  179.1 2.8 collective-permute-start
  181.9 64.5 %collective-permute-done = f32[1280,640]{1,0:T(8,128)S(1)} collective-permute-done((f32[1280,640]{1,0:T(8,128)S(1)}, f32[1280,640]{1,0:T(8,128)S(1)}, u32[]{:S(2)}, u32[]{:S(2)}) %collective-permute-start) | collective-permute-done | bytes 3276832 | tf_op jit(solution)/shard_map/ppermute | solution.py:51
  246.4 0.3 add.37
  246.7 4.1 %collective-permute-start.1 = (f32[1280,640]{1,0:T(8,128)S(1)}, f32[1280,640]{1,0:T(8,128)}, u32[]{:S(2)}, u32[]{:S(2)}) collective-permute-start(f32[1280,640]{1,0:T(8,128)S(1)} %add.37), channel_id=1, source_target_pairs={{0,2},{1,3},{2,0},{3,1},{4,6},{5,7},{6,4},{7,5},{8,10},{9,11},{10,... | collective-permute-start | bytes 9830408 | tf_op jit(solution)/shard_map/ppermute | solution.py:51
  250.8 68.2 %collective-permute-done.1 = f32[1280,640]{1,0:T(8,128)} collective-permute-done((f32[1280,640]{1,0:T(8,128)S(1)}, f32[1280,640]{1,0:T(8,128)}, u32[]{:S(2)}, u32[]{:S(2)}) %collective-permute-start.1) | collective-permute-done | bytes 3276832 | tf_op jit(solution)/shard_map/ppermute | solution.py:51
  319.0 3.6 %select_convert_fusion = bf16[1280,640]{1,0:T(8,128)(2,1)} fusion(f32[1280,640]{1,0:T(8,128)S(1)} %add.37, f32[1280,640]{1,0:T(8,128)} %collective-permute-done.1, s32[640]{0:T(1024)S(1)} %iota_add_fusion.1, s32[1280]{0:T(1024)S(1)} %iota_add_fusion), kind=kLoop, calls=%fused_computation | loop fusion | flops 4096000 | bytes 8199680 | tf_op jit(solution)/shard_map/convert_element_type | solution.py:12
  (2 shorter events, 0.0 us)
Async XLA Ops:
  6.5 98.2 %all-gather.5.cloned.1.call-start = ((), (), s32[]{:S(2)}) async-start(), calls=%async_computation.3 | async-start | bytes 2949120 | tf_op jit(solution)/shard_map/all_gather | solution.py:38
  63.0 109.1 %all-gather.3.cloned.1.call-start = ((), (), s32[]{:S(2)}) async-start(), calls=%async_computation.2 | async-start | bytes 5570560 | tf_op jit(solution)/shard_map/all_gather | solution.py:40
  179.1 67.3 %collective-permute-start = (f32[1280,640]{1,0:T(8,128)S(1)}, f32[1280,640]{1,0:T(8,128)S(1)}, u32[]{:S(2)}, u32[]{:S(2)}) collective-permute-start(f32[1280,640]{1,0:T(8,128)S(1)} %fusion), channel_id=1, source_target_pairs={{0,1},{1,0},{2,3},{3,2},{4,5},{5,4},{6,7},{7,6},{8,9},{9,8},{10,11... | collective-permute-start | bytes 9830408 | tf_op jit(solution)/shard_map/ppermute | solution.py:51
  246.7 72.3 %collective-permute-start.1 = (f32[1280,640]{1,0:T(8,128)S(1)}, f32[1280,640]{1,0:T(8,128)}, u32[]{:S(2)}, u32[]{:S(2)}) collective-permute-start(f32[1280,640]{1,0:T(8,128)S(1)} %add.37), channel_id=1, source_target_pairs={{0,2},{1,3},{2,0},{3,1},{4,6},{5,7},{6,4},{7,5},{8,10},{9,11},{10,... | collective-permute-start | bytes 9830408 | tf_op jit(solution)/shard_map/ppermute | solution.py:51
Sparse Core Ops, SparseCore 0:
  63.1 29.0 all-gather.4
  104.8 67.1 all-gather.2
